TPU v7x, 32 devices: a whole 2x2x4 slice. The times are simulated.
32 devices in a mesh: dp: 8 (over y, x, core), tensor: 4 (over z).
Axes of the slice: x: 2, y: 2, z: 4, core: 2. Of those that a mesh axis runs over, the one named last changes fastest.
Arguments:
- inputs: bfloat16 [8192, 1536], P(('dp', 'tensor')), may hold values from -12 to 12
- norm1_gain: float32 [1536], replicated, may hold values from 0.5 to 1.5
- w_in_x: bfloat16 [1536, 2048], P('dp', 'tensor'), may hold values from -0.15625 to 0.15625
- w_in_y: bfloat16 [1536, 2048], P('dp', 'tensor'), may hold values from -0.15625 to 0.15625
- conv_w: float32 [4, 2048], P(None, 'tensor'), may hold values from -3 to 3
- conv_b: float32 [2048], P('tensor'), may hold values from -1.8 to 1.8
- gates: bfloat16 [2, 16, 128, 128], P(None, 'tensor', 'dp'), may hold values from -0.5 to 0.5
- gate_bias: float32 [2, 2048], P(None, 'tensor'), may hold values from -1 to 1
- decay_param: float32 [2048], P('tensor'), may hold values from -7 to -1
- w_out: bfloat16 [1536, 2048], P('dp', 'tensor'), may hold values from -0.375 to 0.375
- norm2_gain: float32 [1536], replicated, may hold values from 0.5 to 1.5
- w_gate: bfloat16 [1536, 4608], P('dp', 'tensor'), may hold values from -0.15625 to 0.15625
- w_up: bfloat16 [1536, 4608], P('dp', 'tensor'), may hold values from -0.15625 to 0.15625
- w_down: bfloat16 [1536, 4608], P('dp', 'tensor'), may hold values from -0.125 to 0.125
- cotangent: bfloat16 [8192, 1536], P(('dp', 'tensor')), may hold values from -6 to 6
Outputs:
- output: bfloat16 [8192, 1536], P(('dp', 'tensor'))
- grad_inputs: bfloat16 [8192, 1536], P(('dp', 'tensor'))
- grad_norm1_gain: float32 [1536], replicated
- grad_w_in_x: float32 [1536, 2048], P('dp', 'tensor')
- grad_w_in_y: float32 [1536, 2048], P('dp', 'tensor')
- grad_conv_w: float32 [4, 2048], replicated
- grad_conv_b: float32 [2048], replicated
- grad_gates: float32 [2, 16, 128, 128], P(None, 'tensor', 'dp')
- grad_gate_bias: float32 [2, 2048], replicated
- grad_decay_param: float32 [2048], replicated
- grad_w_out: float32 [1536, 2048], P('dp', 'tensor')
- grad_norm2_gain: float32 [1536], replicated
- grad_w_gate: float32 [1536, 4608], P('dp', 'tensor')
- grad_w_up: float32 [1536, 4608], P('dp', 'tensor')
- grad_w_down: float32 [1536, 4608], P('dp', 'tensor')
- stream_rms: float32 [4], replicated
All inputs are finite; a program needn't handle non-finite values.
Results may differ from a plain program's by a relative error of at most 0.0085.
Values may be sent and summed in bfloat16 or wider, within the bound.
A program may use at most 192 MiB of HBM per device.

v0:
```python
import jax
import jax.numpy as jnp
from jax import lax
from jax.sharding import PartitionSpec as P

CONV = 4
SEQ_LEN = 1024
epsilon = 1e-06


def gelu_tanh(value):
    return jax.nn.gelu(value, approximate=True)


def combine(earlier, later):
    return (earlier[0] * later[0], later[0] * earlier[1] + later[1])


def norm_back(value, scale, gain, grad):
    scaled = gain * grad
    return scale * scaled - value * scale * scale * scale * jnp.mean(
        scaled * value, axis=1, keepdims=True
    )


def row_product(left, right):
    return lax.dot_general(
        left, right, (((0,), (0,)), ((), ())), preferred_element_type=jnp.float32
    )


def back_product(left, right):
    return lax.dot_general(
        left, right, (((1,), (1,)), ((), ())), preferred_element_type=jnp.float32
    )


def local(
    inputs,
    norm1_gain,
    w_in_x,
    w_in_y,
    conv_w,
    conv_b,
    gates,
    gate_bias,
    decay_param,
    w_out,
    norm2_gain,
    w_gate,
    w_up,
    w_down,
    cotangent,
):
    row_count = inputs.shape[0]
    model_width = inputs.shape[1]
    tensor_count = lax.axis_size("tensor")
    group_rows = row_count * tensor_count
    seq_count = group_rows // SEQ_LEN
    rec_x, rec_y, rec_o, gate_mats = (
        lax.all_gather(w_in_x, "dp", axis=0, tiled=True),
        lax.all_gather(w_in_y, "dp", axis=0, tiled=True),
        lax.all_gather(w_out, "dp", axis=0, tiled=True),
        lax.all_gather(gates, "dp", axis=2, tiled=True),
    )
    channels = rec_x.shape[1]
    blocks_here = gate_mats.shape[1]
    block_width = gate_mats.shape[3]
    residual = inputs.astype(jnp.float32)
    scale_one = lax.rsqrt(jnp.mean(residual * residual, axis=1, keepdims=True) + epsilon)
    n_one = (residual * scale_one * norm1_gain).astype(jnp.bfloat16)
    full_one = lax.all_gather(n_one, "tensor", axis=0, tiled=True)
    x_branch = jnp.dot(full_one, rec_x, preferred_element_type=jnp.float32)
    y_pre = jnp.dot(full_one, rec_y, preferred_element_type=jnp.float32)
    seq_x = x_branch.reshape(seq_count, SEQ_LEN, channels)
    padded = jnp.pad(seq_x, ((0, 0), (CONV - 1, 0), (0, 0)))
    conv_sum = conv_b + jnp.zeros_like(seq_x)
    for k in range(CONV):
        conv_sum = conv_sum + conv_w[k] * padded[:, CONV - 1 - k : CONV - 1 - k + SEQ_LEN]
    conv_low = conv_sum.reshape(group_rows, channels).astype(jnp.bfloat16)
    conv_value = conv_low.astype(jnp.float32)
    blocked = conv_low.reshape(group_rows, blocks_here, block_width)
    z_input = (
        jnp.einsum(
            "gbi,bij->gbj", blocked, gate_mats[0], preferred_element_type=jnp.float32
        ).reshape(group_rows, channels)
        + gate_bias[0]
    )
    z_decay = (
        jnp.einsum(
            "gbi,bij->gbj", blocked, gate_mats[1], preferred_element_type=jnp.float32
        ).reshape(group_rows, channels)
        + gate_bias[1]
    )
    seq_start = (jnp.arange(group_rows) % SEQ_LEN == 0)[:, None]

    def coefficients(input_pre, decay_pre, conv_part, decay_raw):
        log_decay = -8.0 * jax.nn.sigmoid(decay_pre) * jax.nn.softplus(decay_raw)
        mult = jnp.where(seq_start, 1.0, jnp.sqrt(-jnp.expm1(2.0 * log_decay)))
        return (jnp.exp(log_decay), mult * jax.nn.sigmoid(input_pre) * conv_part)

    (decays, inflow), pull_coeff = jax.vjp(coefficients, z_input, z_decay, conv_value, decay_param)
    seq_decay = decays.reshape(seq_count, SEQ_LEN, channels)
    _, seq_states = lax.associative_scan(
        combine, (seq_decay, inflow.reshape(seq_count, SEQ_LEN, channels)), axis=1
    )
    states = seq_states.reshape(group_rows, channels)
    y_gate = gelu_tanh(y_pre)
    mixed_out = (states * y_gate).astype(jnp.bfloat16)
    branch = lax.psum_scatter(
        back_product(mixed_out, rec_o), "tensor", scatter_dimension=0, tiled=True
    )
    stream = residual + branch
    mlp_g, mlp_u, mlp_d = (
        lax.all_gather(w_gate, "dp", axis=0, tiled=True),
        lax.all_gather(w_up, "dp", axis=0, tiled=True),
        lax.all_gather(w_down, "dp", axis=0, tiled=True),
    )
    scale_two = lax.rsqrt(jnp.mean(stream * stream, axis=1, keepdims=True) + epsilon)
    n_two = (stream * scale_two * norm2_gain).astype(jnp.bfloat16)
    full_two = lax.all_gather(n_two, "tensor", axis=0, tiled=True)
    gate_pre = jnp.dot(full_two, mlp_g, preferred_element_type=jnp.float32)
    up_pre = jnp.dot(full_two, mlp_u, preferred_element_type=jnp.float32)
    hidden = (gelu_tanh(gate_pre) * up_pre).astype(jnp.bfloat16)
    ffn_out = lax.psum_scatter(
        back_product(hidden, mlp_d), "tensor", scatter_dimension=0, tiled=True
    )
    result = stream + ffn_out
    output = result.astype(jnp.bfloat16)
    squares = jnp.stack(
        [
            jnp.sum(stream * stream),
            jnp.sum(branch * branch),
            jnp.sum(ffn_out * ffn_out),
            jnp.sum(result * result),
        ]
    )
    upstream = cotangent.astype(jnp.float32)
    full_cot = lax.all_gather(cotangent, "tensor", axis=0, tiled=True)
    d_hidden = jnp.dot(full_cot, mlp_d, preferred_element_type=jnp.float32)
    grad_down = row_product(full_cot, hidden)
    _, pull_mlp = jax.vjp(
        lambda gate_value, up_value: gelu_tanh(gate_value) * up_value, gate_pre, up_pre
    )
    d_gate, d_up = pull_mlp(d_hidden)
    d_gate_low = d_gate.astype(jnp.bfloat16)
    d_up_low = d_up.astype(jnp.bfloat16)
    grad_gate_w = row_product(full_two, d_gate_low)
    grad_up_w = row_product(full_two, d_up_low)
    d_two = lax.psum_scatter(
        back_product(d_gate_low, mlp_g) + back_product(d_up_low, mlp_u),
        "tensor",
        scatter_dimension=0,
        tiled=True,
    )
    grad_gain_two = jnp.sum(d_two * stream * scale_two, axis=0)
    d_stream = upstream + norm_back(stream, scale_two, norm2_gain, d_two)
    mlp_summed = (grad_gate_w, grad_up_w, grad_down)
    full_branch = lax.all_gather(d_stream.astype(jnp.bfloat16), "tensor", axis=0, tiled=True)
    d_mixed = jnp.dot(full_branch, rec_o, preferred_element_type=jnp.float32)
    grad_out_w = row_product(full_branch, mixed_out)
    d_states = d_mixed * y_gate
    _, pull_gelu = jax.vjp(gelu_tanh, y_pre)
    d_y_low = pull_gelu(d_mixed * states)[0].astype(jnp.bfloat16)
    next_decay = jnp.concatenate([seq_decay[:, 1:], jnp.zeros_like(seq_decay[:, :1])], axis=1)
    _, carried = lax.associative_scan(
        combine, (next_decay, d_states.reshape(seq_count, SEQ_LEN, channels)), reverse=True, axis=1
    )
    prev_states = jnp.concatenate([jnp.zeros_like(seq_states[:, :1]), seq_states[:, :-1]], axis=1)
    d_decays = (carried * prev_states).reshape(group_rows, channels)
    d_input_pre, d_decay_pre, d_conv_direct, grad_decay = pull_coeff(
        (d_decays, carried.reshape(group_rows, channels))
    )
    d_input_low = d_input_pre.astype(jnp.bfloat16)
    d_decay_low = d_decay_pre.astype(jnp.bfloat16)
    grad_bias = jnp.stack(
        [
            jnp.sum(d_input_low, axis=0, dtype=jnp.float32),
            jnp.sum(d_decay_low, axis=0, dtype=jnp.float32),
        ]
    )
    input_blocks = d_input_low.reshape(group_rows, blocks_here, block_width)
    decay_blocks = d_decay_low.reshape(group_rows, blocks_here, block_width)
    grad_gate_mats = jnp.stack(
        [
            jnp.einsum("gbi,gbj->bij", blocked, input_blocks, preferred_element_type=jnp.float32),
            jnp.einsum("gbi,gbj->bij", blocked, decay_blocks, preferred_element_type=jnp.float32),
        ]
    )
    d_conv = d_conv_direct + jnp.einsum(
        "gbj,bij->gbi", input_blocks, gate_mats[0], preferred_element_type=jnp.float32
    ).reshape(group_rows, channels)
    d_conv = d_conv + jnp.einsum(
        "gbj,bij->gbi", decay_blocks, gate_mats[1], preferred_element_type=jnp.float32
    ).reshape(group_rows, channels)
    seq_dconv = d_conv.reshape(seq_count, SEQ_LEN, channels)
    grad_conv_b = jnp.sum(seq_dconv, axis=(0, 1))
    padded_back = jnp.pad(seq_dconv, ((0, 0), (0, CONV - 1), (0, 0)))
    tap_grads = []
    d_x_seq = jnp.zeros_like(seq_dconv)
    for k in range(CONV):
        tap_grads.append(
            jnp.sum(seq_dconv * padded[:, CONV - 1 - k : CONV - 1 - k + SEQ_LEN], axis=(0, 1))
        )
        d_x_seq = d_x_seq + conv_w[k] * padded_back[:, k : k + SEQ_LEN]
    grad_conv_w = jnp.stack(tap_grads)
    d_x_low = d_x_seq.reshape(group_rows, channels).astype(jnp.bfloat16)
    grad_in_x_w = row_product(full_one, d_x_low)
    grad_in_y_w = row_product(full_one, d_y_low)
    d_one = lax.psum_scatter(
        back_product(d_x_low, rec_x) + back_product(d_y_low, rec_y),
        "tensor",
        scatter_dimension=0,
        tiled=True,
    )
    grad_gain_one = jnp.sum(d_one * residual * scale_one, axis=0)
    grad_inputs = (d_stream + norm_back(residual, scale_one, norm1_gain, d_one)).astype(
        jnp.bfloat16
    )
    small_grads = jnp.concatenate(
        [grad_conv_w, grad_conv_b[None], grad_bias, grad_decay[None]], axis=0
    )
    spread_grads = lax.dynamic_update_slice(
        jnp.zeros((small_grads.shape[0], channels * tensor_count), jnp.float32),
        small_grads,
        (0, lax.axis_index("tensor") * channels),
    )
    gain_total, small_total, square_total = lax.psum(
        (jnp.stack([grad_gain_one, grad_gain_two]), spread_grads, squares), ("dp", "tensor")
    )
    stream_rms = jnp.sqrt(
        square_total / (row_count * lax.axis_size("dp") * tensor_count * model_width)
    )
    summed_all = (
        lax.psum_scatter(grad_in_x_w, "dp", scatter_dimension=0, tiled=True),
        lax.psum_scatter(grad_in_y_w, "dp", scatter_dimension=0, tiled=True),
        lax.psum_scatter(grad_out_w, "dp", scatter_dimension=0, tiled=True),
        lax.psum_scatter(grad_gate_mats, "dp", scatter_dimension=2, tiled=True),
        lax.psum_scatter(mlp_summed[0], "dp", scatter_dimension=0, tiled=True),
        lax.psum_scatter(mlp_summed[1], "dp", scatter_dimension=0, tiled=True),
        lax.psum_scatter(mlp_summed[2], "dp", scatter_dimension=0, tiled=True),
    )
    rec_summed = summed_all[:4]
    grad_gate_sum, grad_up_sum, grad_down_sum = (summed_all[4], summed_all[5], summed_all[6])
    return (
        output,
        grad_inputs,
        gain_total[0],
        rec_summed[0],
        rec_summed[1],
        small_total[0:CONV],
        small_total[CONV],
        rec_summed[3],
        small_total[CONV + 1 : CONV + 3],
        small_total[CONV + 3],
        rec_summed[2],
        gain_total[1],
        grad_gate_sum,
        grad_up_sum,
        grad_down_sum,
        stream_rms,
    )


def solution(mesh):
    return jax.shard_map(
        local,
        mesh=mesh,
        in_specs=(
            P(("dp", "tensor"), None),
            P(),
            P("dp", "tensor"),
            P("dp", "tensor"),
            P(None, "tensor"),
            P("tensor"),
            P(None, "tensor", "dp", None),
            P(None, "tensor"),
            P("tensor"),
            P("dp", "tensor"),
            P(),
            P("dp", "tensor"),
            P("dp", "tensor"),
            P("dp", "tensor"),
            P(("dp", "tensor"), None),
        ),
        out_specs=(
            P(("dp", "tensor"), None),
            P(("dp", "tensor"), None),
            P(),
            P("dp", "tensor"),
            P("dp", "tensor"),
            P(),
            P(),
            P(None, "tensor", "dp", None),
            P(),
            P(),
            P("dp", "tensor"),
            P(),
            P("dp", "tensor"),
            P("dp", "tensor"),
            P("dp", "tensor"),
            P(),
        ),
        check_vma=False,
    )
```

profile of v0, /device:TPU:0, one launch (start us, length us, event | category | flops | bytes accessed | tf_op | source)
XLA Modules:
  0.0 1922.4 jit_solution(16737749595569484958)
XLA Ops:
  13.7 11.2 all_gather.35
  26.0 12.7 all-gather.13.cloned.1.call-done
  38.7 65.7 %all-gather.11.cloned.1.call-done = bf16[1024,1536]{1,0:T(8,128)(2,1)} async-done(((bf16[256,1536]{1,0:T(8,128)(2,1)}), bf16[1024,1536]{1,0:T(8,128)(2,1)}) %all-gather.11.cloned.1.call-update) | async-done | bytes 3145744 | tf_op jit(solution)/shard_map/all_gather | solution.py:72
  118.9 5.9 fusion.69
  124.8 6.3 slice.563
  131.1 6.3 slice.564
  137.3 6.3 slice.562
  143.6 6.2 slice.566
  257.9 6.4 slice.561
  264.3 6.3 slice.634
  307.0 8.6 pad.152
  319.4 8.7 pad.151
  328.1 7.5 fusion.34
  335.6 6.3 fusion.130
  342.5 108.9 %reduce-scatter.14.cloned.1.call-done = f32[256,1536]{1,0:T(8,128)} async-done(((f32[1024,1536]{1,0:T(8,128)}), f32[256,1536]{1,0:T(8,128)}) %reduce-scatter.14.cloned.1.call-update) | async-done | bytes 1572880 | tf_op jit(solution)/shard_map/reduce_scatter | solution.py:110
  458.6 29.1 %all-gather.21.cloned.1.call-done = bf16[1536,1152]{1,0:T(8,128)(2,1)} async-done(((bf16[192,1152]{1,0:T(8,128)(2,1)}), bf16[1536,1152]{1,0:T(8,128)(2,1)}) %all-gather.21.cloned.1.call-update) | async-done | bytes 3538960 | tf_op jit(solution)/shard_map/all_gather | solution.py:115
  487.7 65.7 %all-gather.19.cloned.1.call-done = bf16[1024,1536]{1,0:T(8,128)(2,1)} async-done(((bf16[256,1536]{1,0:T(8,128)(2,1)}), bf16[1024,1536]{1,0:T(8,128)(2,1)}) %all-gather.19.cloned.1.call-update) | async-done | bytes 3145744 | tf_op jit(solution)/shard_map/all_gather | solution.py:121
  553.4 9.3 fusion.131
  562.7 25.2 %all-gather.23.cloned.1.call-done = bf16[1536,1152]{1,0:T(8,128)(2,1)} async-done(((bf16[192,1152]{1,0:T(8,128)(2,1)}), bf16[1536,1152]{1,0:T(8,128)(2,1)}) %all-gather.23.cloned.1.call-update) | async-done | bytes 3538960 | tf_op jit(solution)/shard_map/all_gather | solution.py:116
  587.9 9.4 fusion.132
  597.3 55.7 %all-gather.27.cloned.1.call-done = bf16[1024,1536]{1,0:T(8,128)(2,1)} async-done(((bf16[256,1536]{1,0:T(8,128)(2,1)}), bf16[1024,1536]{1,0:T(8,128)(2,1)}) %all-gather.27.cloned.1.call-update) | async-done | bytes 3145744 | tf_op jit(solution)/shard_map/all_gather | solution.py:139
  653.0 34.4 %all-gather.25.cloned.1.call-done = bf16[1536,1152]{1,0:T(8,128)(2,1)} async-done(((bf16[192,1152]{1,0:T(8,128)(2,1)}), bf16[1536,1152]{1,0:T(8,128)(2,1)}) %all-gather.25.cloned.1.call-update) | async-done | bytes 3538960 | tf_op jit(solution)/shard_map/all_gather | solution.py:117
  687.4 13.0 multiply_convert_fusion
  704.8 6.3 convolution_add_fusion.1
  711.1 9.6 fusion.133
  720.8 101.2 %reduce-scatter.18.cloned.1.call-done = f32[256,1536]{1,0:T(8,128)} async-done(((f32[1024,1536]{1,0:T(8,128)}), f32[256,1536]{1,0:T(8,128)}) %reduce-scatter.18.cloned.1.call-update) | async-done | bytes 1572880 | tf_op jit(solution)/shard_map/reduce_scatter | solution.py:150
  822.0 113.4 %reduce-scatter.16.cloned.1.call-done = f32[256,1536]{1,0:T(8,128)} async-done(((f32[1024,1536]{1,0:T(8,128)}), f32[256,1536]{1,0:T(8,128)}) %reduce-scatter.16.cloned.1.call-update) | async-done | bytes 1572880 | tf_op jit(solution)/shard_map/reduce_scatter | solution.py:125
  935.5 5.2 multiply_reduce_fusion.9
  945.5 6.5 slice.639
  952.0 6.3 slice.644
  958.3 6.2 slice.637
  964.5 8.9 slice.640
  973.4 8.9 slice.645
  982.3 9.2 slice.638
  1000.2 6.1 all-gather.29.cloned.1.call-done
  1006.3 8.9 fusion.25
  1015.3 16.6 reverse.6
  1031.9 6.3 slice.641
  1038.2 6.2 slice.642
  1153.8 6.3 slice.713
  1184.6 4.7 pad.169
  1196.7 8.6 pad.172
  1209.1 8.7 pad.171
  1221.8 16.7 rev.8
  1248.4 7.0 convert_reduce_fusion.1
  1270.5 8.6 multiply_reduce_fusion.1
  1280.5 5.0 convert_reduce_fusion
  1299.3 9.9 fusion.137
  1309.3 9.9 fusion.138
  1319.4 9.4 convolution_bitcast_fusion
  1328.8 8.1 copy.95
  1339.9 5.3 fusion.60
  1347.2 4.7 fusion.136
  1353.1 5.4 fusion.135
  1362.0 40.5 %all-reduce.47.cloned.1.call-done = f32[8,2048]{1,0:T(8,128)} async-done(((f32[8,2048]{1,0:T(8,128)}), f32[8,2048]{1,0:T(8,128)}) %all-reduce.47.cloned.1.call-update) | async-done | bytes 65552 | tf_op jit(solution)/shard_map/psum | solution.py:228
  1407.0 109.3 %reduce-scatter.20.cloned.1.call-done = f32[256,1536]{1,0:T(8,128)} async-done(((f32[1024,1536]{1,0:T(8,128)}), f32[256,1536]{1,0:T(8,128)}) %reduce-scatter.20.cloned.1.call-update) | async-done | bytes 1572880 | tf_op jit(solution)/shard_map/reduce_scatter | solution.py:210
  1518.1 41.2 %all-reduce.44 = (f32[2,1536]{1,0:T(2,128)S(1)}, f32[4]{0:T(128)S(1)}) all-reduce(f32[2,1536]{1,0:T(2,128)S(1)} %pad_maximum_fusion.15, f32[4]{0:T(128)S(1)} %pad_maximum_fusion.20), channel_id=1, replica_groups=mesh['dp'=8,'tensor'=4] {'dp','tensor'}, use_global_device_ids=true, to_apply=%region_10.11 | all-reduce | flops 3076 | bytes 24608 | tf_op jit(solution)/shard_map/psum | solution.py:228
  1564.3 22.5 %reduce-scatter.30.cloned.1.call-done = f32[192,1152]{1,0:T(8,128)} async-done(((f32[1536,1152]{1,0:T(8,128)}), f32[192,1152]{1,0:T(8,128)}) %reduce-scatter.30.cloned.1.call-update) | async-done | bytes 884752 | tf_op jit(solution)/shard_map/reduce_scatter | solution.py:239
  1586.9 69.9 %reduce-scatter.32.cloned.1.call-done = f32[192,1152]{1,0:T(8,128)} async-done(((f32[1536,1152]{1,0:T(8,128)}), f32[192,1152]{1,0:T(8,128)}) %reduce-scatter.32.cloned.1.call-update) | async-done | bytes 884752 | tf_op jit(solution)/shard_map/reduce_scatter | solution.py:240
  1656.8 69.5 %reduce-scatter.34.cloned.1.call-done = f32[192,1152]{1,0:T(8,128)} async-done(((f32[1536,1152]{1,0:T(8,128)}), f32[192,1152]{1,0:T(8,128)}) %reduce-scatter.34.cloned.1.call-update) | async-done | bytes 884752
  1726.2 38.1 %reduce-scatter.26.cloned.1.call-done = f32[2,4,16,128]{3,2,1,0:T(8,128)} async-done(((f32[2,4,128,128]{3,2,1,0:T(8,128)}), f32[2,4,16,128]{3,2,1,0:T(8,128)}) %reduce-scatter.26.cloned.1.call-update) | async-done | bytes 65552 | tf_op jit(solution)/shard_map/reduce_scatter | solution.py:238
  1764.3 50.1 %reduce-scatter.22.cloned.1.call-done = f32[192,512]{1,0:T(8,128)} async-done(((f32[1536,512]{1,0:T(8,128)}), f32[192,512]{1,0:T(8,128)}) %reduce-scatter.22.cloned.1.call-update) | async-done | bytes 393232 | tf_op jit(solution)/shard_map/reduce_scatter | solution.py:235
  1814.4 50.6 %reduce-scatter.28.cloned.1.call-done = f32[192,512]{1,0:T(8,128)} async-done(((f32[1536,512]{1,0:T(8,128)}), f32[192,512]{1,0:T(8,128)}) %reduce-scatter.28.cloned.1.call-update) | async-done | bytes 393232 | tf_op jit(solution)/shard_map/reduce_scatter | solution.py:237
  1865.0 50.2 %reduce-scatter.24.cloned.1.call-done = f32[192,512]{1,0:T(8,128)} async-done(((f32[1536,512]{1,0:T(8,128)}), f32[192,512]{1,0:T(8,128)}) %reduce-scatter.24.cloned.1.call-update) | async-done | bytes 393232 | tf_op jit(solution)/shard_map/reduce_scatter | solution.py:236
  (507 shorter events, 405.4 us)
Async XLA Ops:
  7.2 31.5 %all-gather.13.cloned.1.call-start = ((), (), s32[]{:S(2)}) async-start(), calls=%async_computation.12 | async-start | bytes 1769472 | tf_op jit(solution)/shard_map/all_gather | solution.py:61
  7.9 96.4 %all-gather.11.cloned.1.call-start = ((), (), s32[]{:S(2)}) async-start(), calls=%async_computation.11 | async-start | bytes 3932160 | tf_op jit(solution)/shard_map/all_gather | solution.py:72
  9.4 15.9 copy-start.86
  9.4 16.0 copy-start.73
  11.7 316.4 %all-gather.15.cloned.1.call-start = ((), (), s32[]{:S(2)}) async-start(), calls=%async_computation.13 | async-start | bytes 1769472 | tf_op jit(solution)/shard_map/all_gather | solution.py:62
  12.4 323.2 %all-gather.17.cloned.1.call-start = ((), (), s32[]{:S(2)}) async-start(), calls=%async_computation.14 | async-start | bytes 1769472 | tf_op jit(solution)/shard_map/all_gather | solution.py:63
  13.0 438.4 %reduce-scatter.14.cloned.1.call-start = ((), (), s32[]{:S(2)}) async-start(), calls=%async_computation.15 | async-start | bytes 7864320 | tf_op jit(solution)/shard_map/reduce_scatter | solution.py:110
  13.6 94.9 %copy-start.50 = (f32[1,512]{1,0:T(1,128)}, f32[1,512]{1,0:T(1,128)S(1)}, u32[]{:S(2)}) copy-start(f32[1,512]{1,0:T(1,128)S(1)} %get-tuple-element.125) | copy-start | bytes 6148
  13.6 94.9 %copy-start.52 = (f32[1,512]{1,0:T(1,128)}, f32[1,512]{1,0:T(1,128)S(1)}, u32[]{:S(2)}) copy-start(f32[1,512]{1,0:T(1,128)S(1)} %get-tuple-element.126) | copy-start | bytes 6148
  13.6 94.9 %copy-start.54 = (f32[1,512]{1,0:T(1,128)}, f32[1,512]{1,0:T(1,128)S(1)}, u32[]{:S(2)}) copy-start(f32[1,512]{1,0:T(1,128)S(1)} %get-tuple-element.127) | copy-start | bytes 6148
  13.6 94.9 %copy-start.56 = (f32[1,512]{1,0:T(1,128)}, f32[1,512]{1,0:T(1,128)S(1)}, u32[]{:S(2)}) copy-start(f32[1,512]{1,0:T(1,128)S(1)} %get-tuple-element.128) | copy-start | bytes 6148
  25.3 89.0 %copy-start.23 = (bf16[1,4,128,128]{2,3,1,0:T(8,128)(2,1)}, bf16[1,4,128,128]{2,3,1,0:T(8,128)(2,1)S(1)}, u32[]{:S(2)}) copy-start(bf16[1,4,128,128]{2,3,1,0:T(8,128)(2,1)S(1)} %copy.98) | copy-start | bytes 393220
  25.3 93.6 %copy-start.34 = (f32[1,512]{1,0:T(1,128)}, f32[1,512]{1,0:T(1,128)S(1)}, u32[]{:S(2)}) copy-start(f32[1,512]{1,0:T(1,128)S(1)} %get-tuple-element.133) | copy-start | bytes 6148
  25.4 93.6 %copy-start.39 = (f32[1,512]{1,0:T(1,128)}, f32[1,512]{1,0:T(1,128)S(1)}, u32[]{:S(2)}) copy-start(f32[1,512]{1,0:T(1,128)S(1)} %get-tuple-element.134) | copy-start | bytes 6148
  26.0 93.0 %copy-start.41 = (f32[512]{0:T(512)}, f32[512]{0:T(512)S(1)}, u32[]{:S(2)}) copy-start(f32[512]{0:T(512)S(1)} %get-tuple-element.139) | copy-start | bytes 6148
  26.0 83.9 %copy-start.87 = (f32[512]{0:T(512)S(1)}, f32[512]{0:T(512)}, u32[]{:S(2)}) copy-start(f32[512]{0:T(512)} %param.20) | copy-start | bytes 6148
  257.9 14.0 copy-start.60
  257.9 14.0 copy-start.82
  257.9 14.0 copy-start.83
  257.9 14.1 copy-start.44
  257.9 14.1 copy-start.45
  257.9 14.1 copy-start.79
  257.9 14.2 copy-start.36
  257.9 14.2 copy-start.77
  257.9 14.3 copy-start.29
  257.9 14.3 copy-start.30
  257.9 14.3 copy-start.75
  341.9 113.5 %copy-start.28 = (f32[1536]{0:T(1024)S(1)}, f32[1536]{0:T(1024)}, u32[]{:S(2)}) copy-start(f32[1536]{0:T(1024)} %param.25) | copy-start | bytes 18436
  341.9 145.8 %all-gather.21.cloned.1.call-start = ((), (), s32[]{:S(2)}) async-start(), calls=%async_computation.17 | async-start | bytes 3981312 | tf_op jit(solution)/shard_map/all_gather | solution.py:115
  342.5 210.9 %all-gather.19.cloned.1.call-start = ((), (), s32[]{:S(2)}) async-start(), calls=%async_computation.16 | async-start | bytes 3932160 | tf_op jit(solution)/shard_map/all_gather | solution.py:121
  454.2 486.4 %copy-start.48 = (f32[256]{0:T(256)}, f32[256]{0:T(256)S(1)}, u32[]{:S(2)}) copy-start(f32[256]{0:T(256)S(1)} %add_rsqrt_fusion) | copy-start | bytes 3076
  456.5 131.5 %all-gather.23.cloned.1.call-start = ((), (), s32[]{:S(2)}) async-start(), calls=%async_computation.18 | async-start | bytes 3981312 | tf_op jit(solution)/shard_map/all_gather | solution.py:116
  457.2 195.8 %all-gather.27.cloned.1.call-start = ((), (), s32[]{:S(2)}) async-start(), calls=%async_computation.21 | async-start | bytes 3932160 | tf_op jit(solution)/shard_map/all_gather | solution.py:139
  457.9 229.5 %all-gather.25.cloned.1.call-start = ((), (), s32[]{:S(2)}) async-start(), calls=%async_computation.19 | async-start | bytes 3981312 | tf_op jit(solution)/shard_map/all_gather | solution.py:117
  458.5 363.5 %reduce-scatter.18.cloned.1.call-start = ((), (), s32[]{:S(2)}) async-start(), calls=%async_computation.22 | async-start | bytes 7864320 | tf_op jit(solution)/shard_map/reduce_scatter | solution.py:150
  687.4 13.1 copy-start.88
  711.1 224.4 %reduce-scatter.16.cloned.1.call-start = ((), (), s32[]{:S(2)}) async-start(), calls=%async_computation.20 | async-start | bytes 7864320 | tf_op jit(solution)/shard_map/reduce_scatter | solution.py:125
  720.7 285.6 %all-gather.29.cloned.1.call-start = ((), (), s32[]{:S(2)}) async-start(), calls=%async_computation.23 | async-start | bytes 3932160 | tf_op jit(solution)/shard_map/all_gather | solution.py:159
  942.1 460.4 %all-reduce.47.cloned.1.call-start = ((), (), s32[]{:S(2)}) async-start(), calls=%async_computation.27 | async-start | bytes 131072 | tf_op jit(solution)/shard_map/psum | solution.py:228
  1145.0 16.4 copy-start.61
  1145.0 16.4 copy-start.84
  1145.0 16.4 copy-start.85
  1145.0 16.5 copy-start.46
  1145.0 16.5 copy-start.80
  1145.1 16.6 copy-start.37
  1145.1 16.6 copy-start.38
  1145.1 16.6 copy-start.78
  1148.8 12.9 copy-start.32
  1148.8 13.0 copy-start.76
  1286.2 230.1 %reduce-scatter.20.cloned.1.call-start = ((), (), s32[]{:S(2)}) async-start(), calls=%async_computation.24 | async-start | bytes 7864320 | tf_op jit(solution)/shard_map/reduce_scatter | solution.py:210
  1299.3 287.6 %reduce-scatter.30.cloned.1.call-start = ((), (), s32[]{:S(2)}) async-start(), calls=%async_computation.30 | async-start | bytes 7962624 | tf_op jit(solution)/shard_map/reduce_scatter | solution.py:239
  1309.2 347.5 %reduce-scatter.32.cloned.1.call-start = ((), (), s32[]{:S(2)}) async-start(), calls=%async_computation.31 | async-start | bytes 7962624 | tf_op jit(solution)/shard_map/reduce_scatter | solution.py:240
  1319.2 407.1 %reduce-scatter.34.cloned.1.call-start = ((), (), s32[]{:S(2)}) async-start(), calls=%async_computation.32 | async-start | bytes 7962624
  1336.9 427.4 %reduce-scatter.26.cloned.1.call-start = ((), (), s32[]{:S(2)}) async-start(), calls=%async_computation.28 | async-start | bytes 589824 | tf_op jit(solution)/shard_map/reduce_scatter | solution.py:238
  1339.9 474.5 %reduce-scatter.22.cloned.1.call-start = ((), (), s32[]{:S(2)}) async-start(), calls=%async_computation.25 | async-start | bytes 3538944 | tf_op jit(solution)/shard_map/reduce_scatter | solution.py:235
  1345.3 519.7 %reduce-scatter.28.cloned.1.call-start = ((), (), s32[]{:S(2)}) async-start(), calls=%async_computation.29 | async-start | bytes 3538944 | tf_op jit(solution)/shard_map/reduce_scatter | solution.py:237
  1351.9 563.3 %reduce-scatter.24.cloned.1.call-start = ((), (), s32[]{:S(2)}) async-start(), calls=%async_computation.26 | async-start | bytes 3538944 | tf_op jit(solution)/shard_map/reduce_scatter | solution.py:236
  1358.5 157.8 %copy-start.6 = (bf16[256,1536]{1,0:T(8,128)(2,1)S(1)}, bf16[256,1536]{1,0:T(8,128)(2,1)}, u32[]{:S(2)}) copy-start(bf16[256,1536]{1,0:T(8,128)(2,1)} %param.15) | copy-start | bytes 2359300
  1358.5 157.8 %copy-start.33 = (f32[1536]{0:T(1024)S(1)}, f32[1536]{0:T(1024)}, u32[]{:S(2)}) copy-start(f32[1536]{0:T(1024)} %param.16) | copy-start | bytes 18436
  1358.5 157.8 %copy-start.63 = (f32[256]{0:T(256)S(1)}, f32[256]{0:T(256)}, u32[]{:S(2)}) copy-start(f32[256]{0:T(256)} %copy-done.62) | copy-start | bytes 3076
  1358.5 202.0 %copy-start.3 = (f32[256,1536]{1,0:T(8,128)S(1)}, f32[256,1536]{1,0:T(8,128)}, u32[]{:S(2)}) copy-start(f32[256,1536]{1,0:T(8,128)} %copy-done.1) | copy-start | bytes 4718596
  1358.5 202.0 %copy-start.19 = (bf16[256,1536]{1,0:T(8,128)(2,1)S(1)}, bf16[256,1536]{1,0:T(8,128)(2,1)}, u32[]{:S(2)}) copy-start(bf16[256,1536]{1,0:T(8,128)(2,1)} %param.29) | copy-start | bytes 2359300
  1358.5 202.0 %copy-start.49 = (f32[256]{0:T(256)S(1)}, f32[256]{0:T(256)}, u32[]{:S(2)}) copy-start(f32[256]{0:T(256)} %copy-done.48) | copy-start | bytes 3076
  1358.5 202.0 %copy-start.65 = (f32[256]{0:T(256)S(1)}, f32[256]{0:T(256)}, u32[]{:S(2)}) copy-start(f32[256]{0:T(256)} %copy-done.64) | copy-start | bytes 3076
  (51 other events, 233.6 us)
Sparse Core Ops, SparseCore 0:
  9.9 28.7 all-gather.12
  40.8 63.4 all-gather.10
  106.3 24.3 all-gather.14
  132.4 25.6 all-gather.16
  342.0 109.3 reduce-scatter.13
  453.2 34.4 all-gather.20
  489.9 63.4 all-gather.18
  555.3 32.6 all-gather.22
  589.5 63.4 all-gather.26
  654.8 32.6 all-gather.24
  711.2 110.7 reduce-scatter.17
  824.2 111.2 reduce-scatter.15
  942.3 64.0 all-gather.28
  1286.3 116.1 all-reduce.46
  1404.7 111.5 reduce-scatter.19
  1520.2 66.5 reduce-scatter.29
  1591.2 65.4 reduce-scatter.31
  1660.7 65.4 reduce-scatter.33
  1730.2 34.1 reduce-scatter.25
  1768.1 46.2 reduce-scatter.21
  1818.7 46.2 reduce-scatter.27
  1868.9 46.2 reduce-scatter.23
where the time goes:
time: 1950 us; the launch traced here: 1920 us
  waiting for transfers between devices  1120 us (57%)
  local copies, waits for them, and re-layouts  442 us (23%)
  other arithmetic  150 us (8%)
  matrix products  138 us (7%)
  blocking collectives  52.4 us (3%)
    slice x63, local copies, waits for them, and re-layouts, local(): lax.associative_scan(combine, (next_decay, d_states.reshape(seq_count, SE...  156 us
    slice x60, local copies, waits for them, and re-layouts, local(): lax.associative_scan(combine, (seq_decay, inflow.reshape(seq_count, SEQ_L...  127 us
    reduce_scatter x1, waiting for transfers between devices, local(): lax.psum_scatter(back_product(hidden, mlp_d), 'tensor', scatter_dimension...  113 us
    reduce_scatter x1, waiting for transfers between devices, local(): lax.psum_scatter(back_product(d_x_low, rec_x) + back_product(d_y_low, rec...  109 us
    reduce_scatter x1, waiting for transfers between devices, local(): lax.psum_scatter(back_product(mixed_out, rec_o), 'tensor', scatter_dimens...  109 us
    reduce_scatter x1, waiting for transfers between devices, local(): lax.psum_scatter(back_product(d_gate_low, mlp_g) + back_product(d_up_low,...  101 us
    unnamed x23, waiting for transfers between devices  74 us
    reduce_scatter x1, waiting for transfers between devices, local(): lax.psum_scatter(mlp_summed[1], 'dp', scatter_dimension=0, tiled=True)  69.9 us
  transfers between devices with their start and end apart: 22, of which 20 were waited for; matrix products, arithmetic and copies ran while one was open for 21% of the time, Pallas kernels for 0%

commit v1 on v0

--- a/solution.py
+++ b/solution.py
@@ -52,6 +52,19 @@
     w_down,
     cotangent,
 ):
+
+    def serve_the_ways(sample):
+        extent = lax.axis_size("tensor")
+        passed = sorted(((ii, (ii + 1) % extent) for ii in range(extent)))
+        small = sample
+        panels = [small]
+        for p in range(1, extent):
+            small = lax.ppermute(small, axis_name="tensor", perm=passed)
+            panels.insert(0, small)
+        new = jnp.concatenate(panels, 0)
+        inter = lax.axis_index("tensor") + 1
+        return jnp.roll(new, inter * sample.shape[0], 0)
+
     row_count = inputs.shape[0]
     model_width = inputs.shape[1]
     tensor_count = lax.axis_size("tensor")
@@ -136,7 +149,7 @@
         ]
     )
     upstream = cotangent.astype(jnp.float32)
-    full_cot = lax.all_gather(cotangent, "tensor", axis=0, tiled=True)
+    full_cot = serve_the_ways(cotangent)
     d_hidden = jnp.dot(full_cot, mlp_d, preferred_element_type=jnp.float32)
     grad_down = row_product(full_cot, hidden)
     _, pull_mlp = jax.vjp(

time: 1950 us -> 1890 us (0.969)
  waiting for transfers between devices: 1120 us -> 1070 us
    ppermute x0 -> x3, waiting for transfers between devices: none -> 78.5 us  [serve_the_ways(): small = lax.ppermute(small, axis_name='tensor', perm=passed)]
    unnamed x23 -> x21, waiting for transfers between devices: 74 us -> 4.03 us
    reduce_scatter x0 -> x1, waiting for transfers between devices: none -> 69.5 us  [local(): lax.psum_scatter(mlp_summed[2], 'dp', scatter_dimension=0, tiled=True)]
    all_gather x1 -> x0, waiting for transfers between devices: 55.7 us -> none  [local(): full_cot = lax.all_gather(cotangent, 'tensor', axis=0, tiled=True)]
    all_gather x1, waiting for transfers between devices: 65.7 us -> 18.9 us  [local(): full_two = lax.all_gather(n_two, 'tensor', axis=0, tiled=True)]
    all_gather x1, waiting for transfers between devices: 29.1 us -> 0.01 us  [local(): lax.all_gather(w_gate, 'dp', axis=0, tiled=True)]
  transfers between devices with their start and end apart: 22 -> 24, of which waited for: 20 -> 21; matrix products, arithmetic and copies ran while one was open for 21% -> 22% of each run, Pallas kernels for 0% -> 0%
where the time goes in v1:
time: 1890 us; the launch traced here: 1860 us
  waiting for transfers between devices  1070 us (57%)
  local copies, waits for them, and re-layouts  437 us (23%)
  other arithmetic  148 us (8%)
  matrix products  138 us (7%)
  blocking collectives  52.6 us (3%)
    slice x63, local copies, waits for them, and re-layouts, local(): lax.associative_scan(combine, (next_decay, d_states.reshape(seq_count, SE...  152 us
    slice x60, local copies, waits for them, and re-layouts, local(): lax.associative_scan(combine, (seq_decay, inflow.reshape(seq_count, SEQ_L...  123 us
    reduce_scatter x1, waiting for transfers between devices, local(): lax.psum_scatter(back_product(hidden, mlp_d), 'tensor', scatter_dimension...  114 us
    reduce_scatter x1, waiting for transfers between devices, local(): lax.psum_scatter(back_product(d_x_low, rec_x) + back_product(d_y_low, rec...  109 us
    reduce_scatter x1, waiting for transfers between devices, local(): lax.psum_scatter(back_product(mixed_out, rec_o), 'tensor', scatter_dimens...  109 us
    reduce_scatter x1, waiting for transfers between devices, local(): lax.psum_scatter(back_product(d_gate_low, mlp_g) + back_product(d_up_low,...  101 us
    ppermute x3, waiting for transfers between devices, serve_the_ways(): small = lax.ppermute(small, axis_name='tensor', perm=passed)  78.5 us
    reduce_scatter x1, waiting for transfers between devices, local(): lax.psum_scatter(mlp_summed[1], 'dp', scatter_dimension=0, tiled=True)  69.9 us
  transfers between devices with their start and end apart: 24, of which 21 were waited for; matrix products, arithmetic and copies ran while one was open for 22% of the time, Pallas kernels for 0%

profile of v1, /device:TPU:0, one launch (start us, length us, event | category | flops | bytes accessed | tf_op | source)
XLA Modules:
  0.0 1864.4 jit_solution(3670755815463203147)
XLA Ops:
  13.2 11.4 all_gather.32
  25.6 13.1 all-gather.12.cloned.1.call-done
  38.7 65.7 %all-gather.10.cloned.1.call-done = bf16[1024,1536]{1,0:T(8,128)(2,1)} async-done(((bf16[256,1536]{1,0:T(8,128)(2,1)}), bf16[1024,1536]{1,0:T(8,128)(2,1)}) %all-gather.10.cloned.1.call-update) | async-done | bytes 3145744 | tf_op jit(solution)/shard_map/all_gather | solution.py:85
  118.9 5.8 fusion.73
  124.7 6.2 slice.563
  131.0 6.3 slice.564
  137.2 6.3 slice.562
  143.5 6.2 slice.566
  253.9 6.3 slice.561
  260.2 6.3 slice.634
  301.4 8.6 pad.152
  313.8 8.7 pad.151
  322.5 7.5 fusion.38
  330.0 6.2 fusion.136
  336.8 108.9 %reduce-scatter.12.cloned.1.call-done = f32[256,1536]{1,0:T(8,128)} async-done(((f32[1024,1536]{1,0:T(8,128)}), f32[256,1536]{1,0:T(8,128)}) %reduce-scatter.12.cloned.1.call-update) | async-done | bytes 1572880 | tf_op jit(solution)/shard_map/reduce_scatter | solution.py:123
  453.8 19.8 %collective-permute-done = bf16[256,1536]{1,0:T(8,128)(2,1)S(1)} collective-permute-done((bf16[256,1536]{1,0:T(8,128)(2,1)}, bf16[256,1536]{1,0:T(8,128)(2,1)S(1)}, u32[]{:S(2)}, u32[]{:S(2)}) %collective-permute-start) | collective-permute-done | bytes 786464 | tf_op jit(solution)/shard_map/ppermute | solution.py:62
  474.6 20.4 %collective-permute-done.1 = bf16[256,1536]{1,0:T(8,128)(2,1)} collective-permute-done((bf16[256,1536]{1,0:T(8,128)(2,1)S(1)}, bf16[256,1536]{1,0:T(8,128)(2,1)}, u32[]{:S(2)}, u32[]{:S(2)}) %collective-permute-start.1) | collective-permute-done | bytes 786464 | tf_op jit(solution)/shard_map/ppermute | solution.py:62
  494.9 38.3 %collective-permute-done.2 = bf16[256,1536]{1,0:T(8,128)(2,1)} collective-permute-done((bf16[256,1536]{1,0:T(8,128)(2,1)}, bf16[256,1536]{1,0:T(8,128)(2,1)}, u32[]{:S(2)}, u32[]{:S(2)}) %collective-permute-start.2) | collective-permute-done | bytes 786464 | tf_op jit(solution)/shard_map/ppermute | solution.py:62
  545.4 18.9 %all-gather.18.cloned.1.call-done = bf16[1024,1536]{1,0:T(8,128)(2,1)} async-done(((bf16[256,1536]{1,0:T(8,128)(2,1)}), bf16[1024,1536]{1,0:T(8,128)(2,1)}) %all-gather.18.cloned.1.call-update) | async-done | bytes 3145744 | tf_op jit(solution)/shard_map/all_gather | solution.py:134
  564.4 9.4 fusion.137
  573.8 25.2 %all-gather.22.cloned.1.call-done = bf16[1536,1152]{1,0:T(8,128)(2,1)} async-done(((bf16[192,1152]{1,0:T(8,128)(2,1)}), bf16[1536,1152]{1,0:T(8,128)(2,1)}) %all-gather.22.cloned.1.call-update) | async-done | bytes 3538960 | tf_op jit(solution)/shard_map/all_gather | solution.py:129
  598.9 9.3 fusion.138
  608.3 26.6 %all-gather.24.cloned.1.call-done = bf16[1536,1152]{1,0:T(8,128)(2,1)} async-done(((bf16[192,1152]{1,0:T(8,128)(2,1)}), bf16[1536,1152]{1,0:T(8,128)(2,1)}) %all-gather.24.cloned.1.call-update) | async-done | bytes 3538960 | tf_op jit(solution)/shard_map/all_gather | solution.py:130
  634.8 13.0 multiply_convert_fusion
  652.1 6.2 convolution_add_fusion.1
  658.4 9.7 fusion.139
  668.2 101.1 %reduce-scatter.16.cloned.1.call-done = f32[256,1536]{1,0:T(8,128)} async-done(((f32[1024,1536]{1,0:T(8,128)}), f32[256,1536]{1,0:T(8,128)}) %reduce-scatter.16.cloned.1.call-update) | async-done | bytes 1572880 | tf_op jit(solution)/shard_map/reduce_scatter | solution.py:163
  769.3 113.6 %reduce-scatter.14.cloned.1.call-done = f32[256,1536]{1,0:T(8,128)} async-done(((f32[1024,1536]{1,0:T(8,128)}), f32[256,1536]{1,0:T(8,128)}) %reduce-scatter.14.cloned.1.call-update) | async-done | bytes 1572880 | tf_op jit(solution)/shard_map/reduce_scatter | solution.py:138
  882.9 5.2 multiply_reduce_fusion.9
  893.1 6.5 slice.639
  899.5 6.3 slice.644
  905.8 6.2 slice.637
  912.1 8.9 slice.640
  921.0 8.9 slice.645
  929.9 9.1 slice.638
  947.7 6.1 all-gather.26.cloned.1.call-done
  953.8 9.0 fusion.29
  962.8 16.7 reverse.6
  979.5 6.2 slice.641
  985.7 6.2 slice.642
  1097.5 6.3 slice.713
  1138.7 8.6 pad.172
  1151.1 8.7 pad.171
  1163.9 16.7 rev.8
  1190.5 7.0 convert_reduce_fusion.1
  1212.7 8.7 multiply_reduce_fusion.1
  1222.7 5.0 convert_reduce_fusion
  1228.7 5.0 add_convert_fusion
  1242.0 9.8 fusion.143
  1251.9 9.8 fusion.144
  1262.1 9.7 fusion.7
  1274.9 5.4 fusion.64
  1282.1 4.7 fusion.142
  1288.1 5.4 fusion.141
  1297.0 47.7 %all-reduce.47.cloned.1.call-done = f32[8,2048]{1,0:T(8,128)} async-done(((f32[8,2048]{1,0:T(8,128)}), f32[8,2048]{1,0:T(8,128)}) %all-reduce.47.cloned.1.call-update) | async-done | bytes 65552 | tf_op jit(solution)/shard_map/psum | solution.py:241
  1349.1 109.3 %reduce-scatter.18.cloned.1.call-done = f32[256,1536]{1,0:T(8,128)} async-done(((f32[1024,1536]{1,0:T(8,128)}), f32[256,1536]{1,0:T(8,128)}) %reduce-scatter.18.cloned.1.call-update) | async-done | bytes 1572880 | tf_op jit(solution)/shard_map/reduce_scatter | solution.py:223
  1460.3 41.2 %all-reduce.44 = (f32[2,1536]{1,0:T(2,128)S(1)}, f32[4]{0:T(128)S(1)}) all-reduce(f32[2,1536]{1,0:T(2,128)S(1)} %pad_maximum_fusion.15, f32[4]{0:T(128)S(1)} %pad_maximum_fusion.20), channel_id=1, replica_groups=mesh['dp'=8,'tensor'=4] {'dp','tensor'}, use_global_device_ids=true, to_apply=%region_10.11 | all-reduce | flops 3076 | bytes 24608 | tf_op jit(solution)/shard_map/psum | solution.py:241
  1506.5 22.5 %reduce-scatter.28.cloned.1.call-done = f32[192,1152]{1,0:T(8,128)} async-done(((f32[1536,1152]{1,0:T(8,128)}), f32[192,1152]{1,0:T(8,128)}) %reduce-scatter.28.cloned.1.call-update) | async-done | bytes 884752 | tf_op jit(solution)/shard_map/reduce_scatter | solution.py:252
  1529.0 69.9 %reduce-scatter.30.cloned.1.call-done = f32[192,1152]{1,0:T(8,128)} async-done(((f32[1536,1152]{1,0:T(8,128)}), f32[192,1152]{1,0:T(8,128)}) %reduce-scatter.30.cloned.1.call-update) | async-done | bytes 884752 | tf_op jit(solution)/shard_map/reduce_scatter | solution.py:253
  1598.9 69.5 %reduce-scatter.32.cloned.1.call-done = f32[192,1152]{1,0:T(8,128)} async-done(((f32[1536,1152]{1,0:T(8,128)}), f32[192,1152]{1,0:T(8,128)}) %reduce-scatter.32.cloned.1.call-update) | async-done | bytes 884752 | tf_op jit(solution)/shard_map/reduce_scatter | solution.py:254
  1668.4 37.9 %reduce-scatter.24.cloned.1.call-done = f32[2,4,16,128]{3,2,1,0:T(8,128)} async-done(((f32[2,4,128,128]{3,2,1,0:T(8,128)}), f32[2,4,16,128]{3,2,1,0:T(8,128)}) %reduce-scatter.24.cloned.1.call-update) | async-done | bytes 65552 | tf_op jit(solution)/shard_map/reduce_scatter | solution.py:251
  1706.3 50.2 %reduce-scatter.20.cloned.1.call-done = f32[192,512]{1,0:T(8,128)} async-done(((f32[1536,512]{1,0:T(8,128)}), f32[192,512]{1,0:T(8,128)}) %reduce-scatter.20.cloned.1.call-update) | async-done | bytes 393232 | tf_op jit(solution)/shard_map/reduce_scatter | solution.py:248
  1756.5 50.5 %reduce-scatter.26.cloned.1.call-done = f32[192,512]{1,0:T(8,128)} async-done(((f32[1536,512]{1,0:T(8,128)}), f32[192,512]{1,0:T(8,128)}) %reduce-scatter.26.cloned.1.call-update) | async-done | bytes 393232 | tf_op jit(solution)/shard_map/reduce_scatter | solution.py:250
  1807.0 50.2 %reduce-scatter.22.cloned.1.call-done = f32[192,512]{1,0:T(8,128)} async-done(((f32[1536,512]{1,0:T(8,128)}), f32[192,512]{1,0:T(8,128)}) %reduce-scatter.22.cloned.1.call-update) | async-done | bytes 393232 | tf_op jit(solution)/shard_map/reduce_scatter | solution.py:249
  (527 shorter events, 408.0 us)
Async XLA Ops:
  7.2 31.5 %all-gather.12.cloned.1.call-start = ((), (), s32[]{:S(2)}) async-start(), calls=%async_computation.12 | async-start | bytes 1769472 | tf_op jit(solution)/shard_map/all_gather | solution.py:74
  7.9 96.4 %all-gather.10.cloned.1.call-start = ((), (), s32[]{:S(2)}) async-start(), calls=%async_computation.11 | async-start | bytes 3932160 | tf_op jit(solution)/shard_map/all_gather | solution.py:85
  9.4 15.6 copy-start.91
  9.4 15.6 copy-start.78
  11.7 310.8 %all-gather.14.cloned.1.call-start = ((), (), s32[]{:S(2)}) async-start(), calls=%async_computation.13 | async-start | bytes 1769472 | tf_op jit(solution)/shard_map/all_gather | solution.py:75
  12.4 317.5 %all-gather.16.cloned.1.call-start = ((), (), s32[]{:S(2)}) async-start(), calls=%async_computation.14 | async-start | bytes 1769472 | tf_op jit(solution)/shard_map/all_gather | solution.py:76
  13.0 432.8 %reduce-scatter.12.cloned.1.call-start = ((), (), s32[]{:S(2)}) async-start(), calls=%async_computation.15 | async-start | bytes 7864320 | tf_op jit(solution)/shard_map/reduce_scatter | solution.py:123
  13.1 105.8 %copy-start.63 = (pred[1024]{0:T(1024)(128)(4,1)}, pred[1024]{0:T(1024)(128)(4,1)S(1)}, u32[]{:S(2)}) copy-start(pred[1024]{0:T(1024)(128)(4,1)S(1)} %fusion.92) | copy-start | bytes 3076
  13.1 95.4 %copy-start.55 = (f32[1,512]{1,0:T(1,128)}, f32[1,512]{1,0:T(1,128)S(1)}, u32[]{:S(2)}) copy-start(f32[1,512]{1,0:T(1,128)S(1)} %get-tuple-element.93) | copy-start | bytes 6148
  13.1 95.4 %copy-start.57 = (f32[1,512]{1,0:T(1,128)}, f32[1,512]{1,0:T(1,128)S(1)}, u32[]{:S(2)}) copy-start(f32[1,512]{1,0:T(1,128)S(1)} %get-tuple-element.94) | copy-start | bytes 6148
  13.1 95.4 %copy-start.59 = (f32[1,512]{1,0:T(1,128)}, f32[1,512]{1,0:T(1,128)S(1)}, u32[]{:S(2)}) copy-start(f32[1,512]{1,0:T(1,128)S(1)} %get-tuple-element.95) | copy-start | bytes 6148
  13.1 95.4 %copy-start.61 = (f32[1,512]{1,0:T(1,128)}, f32[1,512]{1,0:T(1,128)S(1)}, u32[]{:S(2)}) copy-start(f32[1,512]{1,0:T(1,128)S(1)} %get-tuple-element.96) | copy-start | bytes 6148
  24.8 87.1 %copy-start.26 = (bf16[1,4,128,128]{2,3,1,0:T(8,128)(2,1)}, bf16[1,4,128,128]{2,3,1,0:T(8,128)(2,1)S(1)}, u32[]{:S(2)}) copy-start(bf16[1,4,128,128]{2,3,1,0:T(8,128)(2,1)S(1)} %copy.93) | copy-start | bytes 393220
  25.0 89.2 %copy-start.28 = (bf16[1,4,128,128]{2,3,1,0:T(8,128)(2,1)}, bf16[1,4,128,128]{2,3,1,0:T(8,128)(2,1)S(1)}, u32[]{:S(2)}) copy-start(bf16[1,4,128,128]{2,3,1,0:T(8,128)(2,1)S(1)} %copy.94) | copy-start | bytes 393220
  25.0 93.9 %copy-start.39 = (f32[1,512]{1,0:T(1,128)}, f32[1,512]{1,0:T(1,128)S(1)}, u32[]{:S(2)}) copy-start(f32[1,512]{1,0:T(1,128)S(1)} %get-tuple-element.101) | copy-start | bytes 6148
  25.0 93.9 %copy-start.44 = (f32[1,512]{1,0:T(1,128)}, f32[1,512]{1,0:T(1,128)S(1)}, u32[]{:S(2)}) copy-start(f32[1,512]{1,0:T(1,128)S(1)} %get-tuple-element.102) | copy-start | bytes 6148
  25.6 93.2 %copy-start.46 = (f32[512]{0:T(512)}, f32[512]{0:T(512)S(1)}, u32[]{:S(2)}) copy-start(f32[512]{0:T(512)S(1)} %get-tuple-element.107) | copy-start | bytes 6148
  25.6 84.2 %copy-start.92 = (f32[512]{0:T(512)S(1)}, f32[512]{0:T(512)}, u32[]{:S(2)}) copy-start(f32[512]{0:T(512)} %param.20) | copy-start | bytes 6148
  253.8 14.1 copy-start.49
  253.8 14.1 copy-start.50
  253.8 14.2 copy-start.84
  253.8 14.2 copy-start.41
  253.8 14.3 copy-start.82
  253.8 14.3 copy-start.34
  253.9 14.3 copy-start.35
  253.9 14.3 copy-start.80
  336.2 113.5 %copy-start.33 = (f32[1536]{0:T(1024)S(1)}, f32[1536]{0:T(1024)}, u32[]{:S(2)}) copy-start(f32[1536]{0:T(1024)} %param.25) | copy-start | bytes 18436
  336.2 209.2 %all-gather.20.cloned.1.call-start = ((), (), s32[]{:S(2)}) async-start(), calls=%async_computation.17 | async-start | bytes 3981312 | tf_op jit(solution)/shard_map/all_gather | solution.py:128
  336.8 227.6 %all-gather.18.cloned.1.call-start = ((), (), s32[]{:S(2)}) async-start(), calls=%async_computation.16 | async-start | bytes 3932160 | tf_op jit(solution)/shard_map/all_gather | solution.py:134
  448.5 439.6 %copy-start.53 = (f32[256]{0:T(256)}, f32[256]{0:T(256)S(1)}, u32[]{:S(2)}) copy-start(f32[256]{0:T(256)S(1)} %add_rsqrt_fusion) | copy-start | bytes 3076
  450.8 148.2 %all-gather.22.cloned.1.call-start = ((), (), s32[]{:S(2)}) async-start(), calls=%async_computation.18 | async-start | bytes 3981312 | tf_op jit(solution)/shard_map/all_gather | solution.py:129
  451.5 183.3 %all-gather.24.cloned.1.call-start = ((), (), s32[]{:S(2)}) async-start(), calls=%async_computation.19 | async-start | bytes 3981312 | tf_op jit(solution)/shard_map/all_gather | solution.py:130
  452.3 317.0 %reduce-scatter.16.cloned.1.call-start = ((), (), s32[]{:S(2)}) async-start(), calls=%async_computation.21 | async-start | bytes 7864320 | tf_op jit(solution)/shard_map/reduce_scatter | solution.py:163
  452.3 21.4 %collective-permute-start = (bf16[256,1536]{1,0:T(8,128)(2,1)}, bf16[256,1536]{1,0:T(8,128)(2,1)S(1)}, u32[]{:S(2)}, u32[]{:S(2)}) collective-permute-start(bf16[256,1536]{1,0:T(8,128)(2,1)} %param.29), channel_id=1, source_target_pairs={{0,1},{1,2},{2,3},{3,0},{4,5},{5,6},{6,7},{7,4},{8,9},{9,10},{10,1... | collective-permute-start | bytes 2359304 | tf_op jit(solution)/shard_map/ppermute | solution.py:62
  474.6 20.4 %collective-permute-start.1 = (bf16[256,1536]{1,0:T(8,128)(2,1)S(1)}, bf16[256,1536]{1,0:T(8,128)(2,1)}, u32[]{:S(2)}, u32[]{:S(2)}) collective-permute-start(bf16[256,1536]{1,0:T(8,128)(2,1)S(1)} %collective-permute-done), channel_id=1, source_target_pairs={{0,1},{1,2},{2,3},{3,0},{4,5},{5,6},{6,7},{7,4},{8,9},{9,10},{10,1... | collective-permute-start | bytes 2359304 | tf_op jit(solution)/shard_map/ppermute | solution.py:62
  494.9 38.3 %collective-permute-start.2 = (bf16[256,1536]{1,0:T(8,128)(2,1)}, bf16[256,1536]{1,0:T(8,128)(2,1)}, u32[]{:S(2)}, u32[]{:S(2)}) collective-permute-start(bf16[256,1536]{1,0:T(8,128)(2,1)} %collective-permute-done.1), channel_id=1, source_target_pairs={{0,1},{1,2},{2,3},{3,0},{4,5},{5,6},{6,7},{7,4},{8,9},{9,10},{10,1... | collective-permute-start | bytes 2359304 | tf_op jit(solution)/shard_map/ppermute | solution.py:62
  494.9 42.5 %copy-start.24 = (bf16[256,1536]{1,0:T(8,128)(2,1)S(1)}, bf16[256,1536]{1,0:T(8,128)(2,1)}, u32[]{:S(2)}) copy-start(bf16[256,1536]{1,0:T(8,128)(2,1)} %copy-done.23) | copy-start | bytes 2359300
  494.9 43.5 %copy-start.11 = (bf16[256,1536]{1,0:T(8,128)(2,1)S(1)}, bf16[256,1536]{1,0:T(8,128)(2,1)}, u32[]{:S(2)}) copy-start(bf16[256,1536]{1,0:T(8,128)(2,1)} %param.29) | copy-start | bytes 2359300
  658.4 224.5 %reduce-scatter.14.cloned.1.call-start = ((), (), s32[]{:S(2)}) async-start(), calls=%async_computation.20 | async-start | bytes 7864320 | tf_op jit(solution)/shard_map/reduce_scatter | solution.py:138
  668.1 285.7 %all-gather.26.cloned.1.call-start = ((), (), s32[]{:S(2)}) async-start(), calls=%async_computation.22 | async-start | bytes 3932160 | tf_op jit(solution)/shard_map/all_gather | solution.py:172
  889.6 455.1 %all-reduce.47.cloned.1.call-start = ((), (), s32[]{:S(2)}) async-start(), calls=%async_computation.26 | async-start | bytes 131072 | tf_op jit(solution)/shard_map/psum | solution.py:241
  1088.7 16.4 copy-start.66
  1088.7 16.4 copy-start.89
  1088.7 16.4 copy-start.90
  1088.7 16.5 copy-start.51
  1088.7 16.5 copy-start.85
  1088.7 16.6 copy-start.42
  1088.7 16.6 copy-start.43
  1088.7 16.6 copy-start.83
  1228.4 230.1 %reduce-scatter.18.cloned.1.call-start = ((), (), s32[]{:S(2)}) async-start(), calls=%async_computation.23 | async-start | bytes 7864320 | tf_op jit(solution)/shard_map/reduce_scatter | solution.py:223
  1242.0 287.1 %reduce-scatter.28.cloned.1.call-start = ((), (), s32[]{:S(2)}) async-start(), calls=%async_computation.29 | async-start | bytes 7962624 | tf_op jit(solution)/shard_map/reduce_scatter | solution.py:252
  1251.9 347.0 %reduce-scatter.30.cloned.1.call-start = ((), (), s32[]{:S(2)}) async-start(), calls=%async_computation.30 | async-start | bytes 7962624 | tf_op jit(solution)/shard_map/reduce_scatter | solution.py:253
  1261.8 406.6 %reduce-scatter.32.cloned.1.call-start = ((), (), s32[]{:S(2)}) async-start(), calls=%async_computation.31 | async-start | bytes 7962624 | tf_op jit(solution)/shard_map/reduce_scatter | solution.py:254
  1271.8 434.5 %reduce-scatter.24.cloned.1.call-start = ((), (), s32[]{:S(2)}) async-start(), calls=%async_computation.27 | async-start | bytes 589824 | tf_op jit(solution)/shard_map/reduce_scatter | solution.py:251
  1274.8 481.7 %reduce-scatter.20.cloned.1.call-start = ((), (), s32[]{:S(2)}) async-start(), calls=%async_computation.24 | async-start | bytes 3538944 | tf_op jit(solution)/shard_map/reduce_scatter | solution.py:248
  1280.3 526.7 %reduce-scatter.26.cloned.1.call-start = ((), (), s32[]{:S(2)}) async-start(), calls=%async_computation.28 | async-start | bytes 3538944 | tf_op jit(solution)/shard_map/reduce_scatter | solution.py:250
  1286.9 570.3 %reduce-scatter.22.cloned.1.call-start = ((), (), s32[]{:S(2)}) async-start(), calls=%async_computation.25 | async-start | bytes 3538944 | tf_op jit(solution)/shard_map/reduce_scatter | solution.py:249
  1293.5 165.0 %copy-start.6 = (bf16[256,1536]{1,0:T(8,128)(2,1)S(1)}, bf16[256,1536]{1,0:T(8,128)(2,1)}, u32[]{:S(2)}) copy-start(bf16[256,1536]{1,0:T(8,128)(2,1)} %param.15) | copy-start | bytes 2359300
  1293.5 165.0 %copy-start.38 = (f32[1536]{0:T(1024)S(1)}, f32[1536]{0:T(1024)}, u32[]{:S(2)}) copy-start(f32[1536]{0:T(1024)} %param.16) | copy-start | bytes 18436
  1293.5 165.0 %copy-start.68 = (f32[256]{0:T(256)S(1)}, f32[256]{0:T(256)}, u32[]{:S(2)}) copy-start(f32[256]{0:T(256)} %copy-done.67) | copy-start | bytes 3076
  1293.5 209.2 %copy-start.3 = (f32[256,1536]{1,0:T(8,128)S(1)}, f32[256,1536]{1,0:T(8,128)}, u32[]{:S(2)}) copy-start(f32[256,1536]{1,0:T(8,128)} %copy-done.1) | copy-start | bytes 4718596
  1293.5 209.2 %copy-start.13 = (bf16[256,1536]{1,0:T(8,128)(2,1)S(1)}, bf16[256,1536]{1,0:T(8,128)(2,1)}, u32[]{:S(2)}) copy-start(bf16[256,1536]{1,0:T(8,128)(2,1)} %param.29) | copy-start | bytes 2359300
  1293.5 209.2 %copy-start.54 = (f32[256]{0:T(256)S(1)}, f32[256]{0:T(256)}, u32[]{:S(2)}) copy-start(f32[256]{0:T(256)} %copy-done.53) | copy-start | bytes 3076
  1293.5 209.1 %copy-start.70 = (f32[256]{0:T(256)S(1)}, f32[256]{0:T(256)}, u32[]{:S(2)}) copy-start(f32[256]{0:T(256)} %copy-done.69) | copy-start | bytes 3076
  (58 other events, 310.4 us)
Sparse Core Ops, SparseCore 0:
  9.9 28.7 all-gather.11
  40.8 63.4 all-gather.9
  106.3 24.3 all-gather.13
  132.4 25.6 all-gather.15
  336.3 109.4 reduce-scatter.11
  447.5 34.4 all-gather.19
  484.2 80.1 all-gather.17
  566.2 32.6 all-gather.21
  600.8 33.9 all-gather.23
  658.5 110.7 reduce-scatter.15
  771.6 111.2 reduce-scatter.13
  889.7 64.0 all-gather.25
  1228.5 116.1 all-reduce.46
  1346.9 111.5 reduce-scatter.17
  1462.4 66.5 reduce-scatter.27
  1533.4 65.4 reduce-scatter.29
  1602.8 65.4 reduce-scatter.31
  1672.2 34.0 reduce-scatter.23
  1710.2 46.2 reduce-scatter.19
  1760.7 46.2 reduce-scatter.25
  1810.9 46.2 reduce-scatter.21
